TPU v7x, 256 devices: a whole 4x4x8 slice. The times are simulated.
256 devices in a mesh: blk: 32 (over x, y, core), slab: 8 (over z).
Axes of the slice: x: 4, y: 4, z: 8, core: 2. Of those that a mesh axis runs over, the one named last changes fastest.
Arguments:
- amplitudes: bfloat16 [960, 32768], P('blk', 'slab'), may hold values from -6 to 6
- ladder_ints: bfloat16 [32768, 32768], P('slab', 'blk'), may hold values from -0.03125 to 0.03125
- cycle_ints: bfloat16 [8, 64, 120, 512], P('slab', 'blk'), may hold values from -0.0625 to 0.0625
- block_dims: int32 [8, 2], replicated, may hold values from 24 to 64, as said below
Outputs:
- ladder_res: bfloat16 [960, 32768], P('slab', 'blk')
- cycle_res: bfloat16 [8, 512, 512], P('slab', 'blk')
Inputs may be any that keep to these rules, and one draw needn't show every extreme that they name: `block_dims`: every block's two sizes lie within the padded size; in every draw some block's first size equals 64 and some block's second size equals 24.
All inputs are finite; a program needn't handle non-finite values.
Results may differ from a plain program's by a relative error of at most 0.0014.
Values may be sent and summed in bfloat16 or wider, within the bound.
A program may use at most 128 MiB of HBM per device.

v0:
```python
import jax
import jax.numpy as jnp
from jax import lax
from jax.sharding import PartitionSpec as P

BS = 64


def block_sizes(block_dims, owner):
    blocks_count = block_dims.shape[0]
    select = owner[:, None] == lax.iota(jnp.int32, blocks_count)[None, :]
    size_first = jnp.sum(jnp.where(select, block_dims[None, :, 0], 0), 1)
    size_second = jnp.sum(jnp.where(select, block_dims[None, :, 1], 0), 1)
    return (size_first, size_second)


def column_valid(block_dims, first_column, column_count):
    column = first_column + lax.iota(jnp.int32, column_count)
    owner = column // (BS * BS)
    size_first, size_second = block_sizes(block_dims, owner)
    return (column // BS % BS < size_first) & (column % BS < size_second)


def local(amplitudes, ladder_ints, cycle_ints, block_dims):
    slab_index = lax.axis_index("slab")
    blk_index = lax.axis_index("blk")
    block_width = amplitudes.shape[1]
    valid = column_valid(block_dims, slab_index * block_width, block_width)
    masked = jnp.where(valid[None, :], amplitudes, jnp.zeros((), amplitudes.dtype))
    gathered = lax.all_gather(masked, "blk", axis=0, tiled=True)
    pair_rows = gathered.shape[0]
    ladder_sum = lax.psum_scatter(
        jnp.dot(gathered, ladder_ints, preferred_element_type=jnp.float32),
        "slab",
        scatter_dimension=0,
        tiled=True,
    )
    out_columns = ladder_ints.shape[1]
    out_valid = column_valid(block_dims, blk_index * out_columns, out_columns)
    ladder_res = jnp.where(out_valid[None, :], ladder_sum, 0.0).astype(jnp.bfloat16)
    occupied = cycle_ints.shape[2]
    j_window = pair_rows // occupied
    columns = lax.all_to_all(masked, "blk", split_axis=1, concat_axis=0, tiled=True)
    c_part = cycle_ints.shape[1]
    amp_part = columns.reshape(occupied, j_window, c_part, BS)
    cycle_term = jnp.einsum(
        "cke,kjcd->ejd", cycle_ints[0], amp_part, preferred_element_type=jnp.float32
    )
    cycle_term = cycle_term.reshape(cycle_term.shape[0], j_window * BS)
    cycle_sum = lax.psum_scatter(cycle_term, "blk", scatter_dimension=0, tiled=True)
    local_rows = cycle_sum.shape[0]
    own_block = jnp.full((1,), slab_index, jnp.int32)
    size_first, size_second = block_sizes(block_dims, own_block)
    row_virtual = (blk_index * local_rows + lax.iota(jnp.int32, local_rows)) % BS
    column_virtual = lax.iota(jnp.int32, j_window * BS) % BS
    allowed = (row_virtual[:, None] < size_first[0]) & (column_virtual[None, :] < size_second[0])
    cycle_res = jnp.where(allowed, cycle_sum, 0.0).astype(jnp.bfloat16)[None]
    return (ladder_res, cycle_res)


def solution(mesh):
    in_specs = (P("blk", "slab"), P("slab", "blk"), P("slab", "blk", None, None), P())
    out_specs = (P("slab", "blk"), P("slab", "blk", None))
    return jax.shard_map(local, mesh=mesh, in_specs=in_specs, out_specs=out_specs, check_vma=False)
```

profile of v0, /device:TPU:32, one launch (start us, length us, event | category | flops | bytes accessed | tf_op | source)
XLA Modules:
  0.0 221.3 jit_solution(12500049500850182487)
XLA Ops:
  7.2 0.0 copy-start
  7.2 0.0 all-gather.3.cloned.1.call-start
  7.2 0.8 slice_bitcast_fusion.1
  8.0 0.1 select_reduce_fusion
  8.2 1.7 fusion.35
  9.9 0.0 all-gather.3.cloned.1.call-update
  9.9 0.0 reduce-scatter.5.cloned.1.call-start
  10.0 1.0 broadcast_select_fusion
  11.0 0.1 copy.13
  11.1 16.1 %all_to_all.16 = bf16[30,32,128]{2,0,1:T(8,128)(2,1)S(1)} all-to-all(bf16[30,32,128]{2,0,1:T(8,128)(2,1)S(1)} %copy.13), channel_id=1, replica_groups=mesh['blk'=32,'slab'=8] {'blk'}, dimensions={1} | all-to-all | bytes 491520 | tf_op jit(solution)/shard_map/all_to_all | solution.py:43
  27.2 0.2 reshape.217
  27.4 0.0 copy-done
  27.4 0.3 fusion
  27.8 1.3 copy.15
  29.1 0.0 reduce-scatter.5.cloned.1.call-update
  29.1 0.0 reduce-scatter.3.cloned.1.call-start
  29.2 41.9 %all-gather.3.cloned.1.call-done = bf16[32,30,4096]{2,1,0:T(8,128)(2,1)} async-done(((bf16[1,30,4096]{2,1,0:T(8,128)(2,1)}), bf16[32,30,4096]{2,1,0:T(8,128)(2,1)}) %all-gather.3.cloned.1.call-update) | async-done | bytes 7864336 | tf_op jit(solution)/shard_map/all_gather | solution.py:30
  71.1 9.5 %reshape.220 = bf16[960,4096]{1,0:T(8,128)(2,1)} reshape(bf16[32,30,4096]{2,1,0:T(8,128)(2,1)} %all-gather.3.cloned.1.call-done) | data formatting | bytes 15728640
  80.7 0.0 copy-start.1
  80.7 14.3 %fusion.32 = f32[960,1024]{1,0:T(8,128)} fusion(bf16[960,4096]{1,0:T(8,128)(2,1)} %reshape.220, bf16[4096,1024]{1,0:T(8,128)(2,1)} %param.5), kind=kOutput, calls=%fused_computation.76 | convolution fusion | flops 8053063680 | bytes 20185088 | tf_op jit(solution)/shard_map/dot_general | solution.py:33
  94.9 0.0 reduce-scatter.3.cloned.1.call-update
  94.9 0.0 copy-done.1
  94.9 0.6 fusion.28
  95.6 0.7 fusion.24
  96.2 0.7 fusion.30
  96.9 0.1 select_reduce_fusion.2
  97.0 62.7 %reduce-scatter.5.cloned.1.call-done = f32[16,512]{1,0:T(8,128)} async-done(((f32[512,512]{1,0:T(8,128)}), f32[16,512]{1,0:T(8,128)}) %reduce-scatter.5.cloned.1.call-update) | async-done | bytes 32784 | tf_op jit(solution)/shard_map/reduce_scatter | solution.py:50
  159.8 1.4 fusion.7
  161.2 51.8 %reduce-scatter.3.cloned.1.call-done = f32[120,1024]{1,0:T(8,128)} async-done(((f32[960,1024]{1,0:T(8,128)}), f32[120,1024]{1,0:T(8,128)}) %reduce-scatter.3.cloned.1.call-update) | async-done | bytes 491536 | tf_op jit(solution)/shard_map/reduce_scatter | solution.py:32
  213.0 1.8 select_convert_fusion
  (6 shorter events, 0.1 us)
Async XLA Ops:
  7.2 20.3 %copy-start = (bf16[1,2,120,512]{3,2,1,0:T(8,128)(2,1)S(1)}, bf16[1,2,120,512]{3,2,1,0:T(8,128)(2,1)}, u32[]{:S(2)}) copy-start(bf16[1,2,120,512]{3,2,1,0:T(8,128)(2,1)} %param.6) | copy-start | bytes 737284
  7.2 63.9 %all-gather.3.cloned.1.call-start = ((), (), s32[]{:S(2)}) async-start(), calls=%async_computation.5 | async-start | bytes 8650752 | tf_op jit(solution)/shard_map/all_gather | solution.py:30
  9.9 149.9 %reduce-scatter.5.cloned.1.call-start = ((), (), s32[]{:S(2)}) async-start(), calls=%async_computation.4 | async-start | bytes 1081344 | tf_op jit(solution)/shard_map/reduce_scatter | solution.py:50
  29.1 183.9 %reduce-scatter.3.cloned.1.call-start = ((), (), s32[]{:S(2)}) async-start(), calls=%async_computation.3 | async-start | bytes 4423680 | tf_op jit(solution)/shard_map/reduce_scatter | solution.py:32
  80.7 14.3 %copy-start.1 = (s32[8,2]{0,1:T(2,128)S(1)}, s32[8,2]{0,1:T(2,128)}, u32[]{:S(2)}) copy-start(s32[8,2]{0,1:T(2,128)} %param.7) | copy-start | bytes 196
Sparse Core Ops, SparseCore 0:
  10.6 60.4 all-gather.2
  74.9 84.8 reduce-scatter.4
  162.5 50.4 reduce-scatter.2
where the time goes:
time: 225 us; the launch traced here: 221 us
  waiting for transfers between devices  157 us (70%)
  blocking collectives  16.1 us (7%)
  matrix products  14.6 us (6%)
  between operations  13.8 us (6%)
  local copies, waits for them, and re-layouts  12 us (5%)
  other arithmetic  8.14 us (4%)
    reduce_scatter x1, waiting for transfers between devices, local(): lax.psum_scatter(cycle_term, 'blk', scatter_dimension=0, tiled=True)  62.7 us
    reduce_scatter x1, waiting for transfers between devices, local(): lax.psum_scatter(jnp.dot(gathered, ladder_ints, preferred_element_type=jn...  51.8 us
    all_gather x1, waiting for transfers between devices, local(): gathered = lax.all_gather(masked, 'blk', axis=0, tiled=True)  41.9 us
    all_to_all x1, blocking collectives, local(): lax.all_to_all(masked, 'blk', split_axis=1, concat_axis=0, tiled=True)  16.1 us
    dot_general x1, matrix products, local(): jnp.dot(gathered, ladder_ints, preferred_element_type=jnp.float32)  14.3 us
    unnamed x6, local copies, waits for them, and re-layouts  9.59 us
  transfers between devices with their start and end apart: 3, of which 3 were waited for; matrix products, arithmetic and copies ran while one was open for 14% of the time, Pallas kernels for 0%

commit v1 on v0

--- a/solution.py
+++ b/solution.py
@@ -40,8 +40,8 @@
     ladder_res = jnp.where(out_valid[None, :], ladder_sum, 0.0).astype(jnp.bfloat16)
     occupied = cycle_ints.shape[2]
     j_window = pair_rows // occupied
-    columns = lax.all_to_all(masked, "blk", split_axis=1, concat_axis=0, tiled=True)
     c_part = cycle_ints.shape[1]
+    columns = lax.dynamic_slice_in_dim(gathered, blk_index * (c_part * BS), c_part * BS, 1)
     amp_part = columns.reshape(occupied, j_window, c_part, BS)
     cycle_term = jnp.einsum(
         "cke,kjcd->ejd", cycle_ints[0], amp_part, preferred_element_type=jnp.float32

time: 225 us -> 234 us (1.040)
  waiting for transfers between devices: 157 us -> 181 us
  blocking collectives: 16.1 us -> 0 us
    all_gather x1, waiting for transfers between devices: 41.9 us -> 61.1 us  [local(): gathered = lax.all_gather(masked, 'blk', axis=0, tiled=True)]
    all_to_all x1 -> x0, blocking collectives: 16.1 us -> none  [local(): lax.all_to_all(masked, 'blk', split_axis=1, concat_axis=0, tiled=True)]
    reduce_scatter x1, waiting for transfers between devices: 62.7 us -> 68.4 us  [local(): lax.psum_scatter(cycle_term, 'blk', scatter_dimension=0, tiled=True)]
    unnamed x6 -> x5, local copies, waits for them, and re-layouts: 9.59 us -> 9.55 us
  transfers between devices with their start and end apart: 3 -> 3, of which waited for: 3 -> 3; matrix products, arithmetic and copies ran while one was open for 14% -> 8% of each run, Pallas kernels for 0% -> 0%
where the time goes in v1:
time: 234 us; the launch traced here: 230 us
  waiting for transfers between devices  181 us (77%)
  matrix products  14.6 us (6%)
  between operations  13.8 us (6%)
  local copies, waits for them, and re-layouts  12.8 us (5%)
  other arithmetic  7.16 us (3%)
    reduce_scatter x1, waiting for transfers between devices, local(): lax.psum_scatter(cycle_term, 'blk', scatter_dimension=0, tiled=True)  68.4 us
    all_gather x1, waiting for transfers between devices, local(): gathered = lax.all_gather(masked, 'blk', axis=0, tiled=True)  61.1 us
    reduce_scatter x1, waiting for transfers between devices, local(): lax.psum_scatter(jnp.dot(gathered, ladder_ints, preferred_element_type=jn...  51.8 us
    dot_general x1, matrix products, local(): jnp.dot(gathered, ladder_ints, preferred_element_type=jnp.float32)  14.3 us
    unnamed x5, local copies, waits for them, and re-layouts  9.55 us
  transfers between devices with their start and end apart: 3, of which 3 were waited for; matrix products, arithmetic and copies ran while one was open for 8% of the time, Pallas kernels for 0%

profile of v1, /device:TPU:32, one launch (start us, length us, event | category | flops | bytes accessed | tf_op | source)
XLA Modules:
  0.0 230.0 jit_solution(7437866823472221384)
XLA Ops:
  7.2 0.0 copy-start
  7.2 0.0 all-gather.3.cloned.1.call-start
  7.3 0.8 slice_bitcast_fusion.1
  8.0 0.1 select_reduce_fusion
  8.2 1.7 select_bitcast_fusion
  9.9 0.0 all-gather.3.cloned.1.call-update
  9.9 0.0 reduce-scatter.5.cloned.1.call-start
  10.0 61.1 %all-gather.3.cloned.1.call-done = bf16[32,30,4096]{2,1,0:T(8,128)(2,1)} async-done(((bf16[1,30,4096]{2,1,0:T(8,128)(2,1)}), bf16[32,30,4096]{2,1,0:T(8,128)(2,1)}) %all-gather.3.cloned.1.call-update) | async-done | bytes 7864336 | tf_op jit(solution)/shard_map/all_gather | solution.py:30
  71.1 9.5 %reshape.216 = bf16[960,4096]{1,0:T(8,128)(2,1)} reshape(bf16[32,30,4096]{2,1,0:T(8,128)(2,1)} %all-gather.3.cloned.1.call-done) | data formatting | bytes 15728640
  80.7 1.0 constant_dynamic-slice_fusion
  81.6 0.2 reshape.213
  81.8 0.0 copy-done
  81.9 0.3 fusion
  82.2 1.3 copy.12
  83.5 0.0 reduce-scatter.5.cloned.1.call-update
  83.5 0.0 copy-start.1
  83.6 0.0 reduce-scatter.3.cloned.1.call-start
  83.6 14.3 %fusion.32 = f32[960,1024]{1,0:T(8,128)} fusion(bf16[960,4096]{1,0:T(8,128)(2,1)} %reshape.216, bf16[4096,1024]{1,0:T(8,128)(2,1)} %param.5), kind=kOutput, calls=%fused_computation.77 | convolution fusion | flops 8053063680 | bytes 20185088 | tf_op jit(solution)/shard_map/dot_general | solution.py:33
  97.9 0.0 reduce-scatter.3.cloned.1.call-update
  97.9 0.0 copy-done.1
  97.9 0.6 fusion.28
  98.5 0.7 fusion.24
  99.2 0.7 fusion.30
  99.9 0.1 select_reduce_fusion.2
  100.0 68.4 %reduce-scatter.5.cloned.1.call-done = f32[16,512]{1,0:T(8,128)} async-done(((f32[512,512]{1,0:T(8,128)}), f32[16,512]{1,0:T(8,128)}) %reduce-scatter.5.cloned.1.call-update) | async-done | bytes 32784 | tf_op jit(solution)/shard_map/reduce_scatter | solution.py:50
  168.5 1.4 fusion.7
  169.9 51.8 %reduce-scatter.3.cloned.1.call-done = f32[120,1024]{1,0:T(8,128)} async-done(((f32[960,1024]{1,0:T(8,128)}), f32[120,1024]{1,0:T(8,128)}) %reduce-scatter.3.cloned.1.call-update) | async-done | bytes 491536 | tf_op jit(solution)/shard_map/reduce_scatter | solution.py:32
  221.7 1.8 select_convert_fusion
  (4 shorter events, 0.1 us)
Async XLA Ops:
  7.2 74.7 %copy-start = (bf16[1,2,120,512]{3,2,1,0:T(8,128)(2,1)S(1)}, bf16[1,2,120,512]{3,2,1,0:T(8,128)(2,1)}, u32[]{:S(2)}) copy-start(bf16[1,2,120,512]{3,2,1,0:T(8,128)(2,1)} %param.6) | copy-start | bytes 737284
  7.2 63.9 %all-gather.3.cloned.1.call-start = ((), (), s32[]{:S(2)}) async-start(), calls=%async_computation.4 | async-start | bytes 8650752 | tf_op jit(solution)/shard_map/all_gather | solution.py:30
  9.9 158.5 %reduce-scatter.5.cloned.1.call-start = ((), (), s32[]{:S(2)}) async-start(), calls=%async_computation.3 | async-start | bytes 1081344 | tf_op jit(solution)/shard_map/reduce_scatter | solution.py:50
  83.5 14.4 %copy-start.1 = (s32[8,2]{0,1:T(2,128)S(1)}, s32[8,2]{0,1:T(2,128)}, u32[]{:S(2)}) copy-start(s32[8,2]{0,1:T(2,128)} %param.7) | copy-start | bytes 196
  83.6 138.2 %reduce-scatter.3.cloned.1.call-start = ((), (), s32[]{:S(2)}) async-start(), calls=%async_computation.2 | async-start | bytes 4423680 | tf_op jit(solution)/shard_map/reduce_scatter | solution.py:32
Sparse Core Ops, SparseCore 0:
  10.6 60.4 all-gather.2
  83.7 84.7 reduce-scatter.4
  171.2 50.4 reduce-scatter.2

commit v2 on v1

v2 whole, which is shorter than its diff:
```python
import functools

import jax
import jax.numpy as jnp
from jax import lax
from jax.experimental import pallas as pl
from jax.experimental.pallas import tpu as pltpu
from jax.sharding import PartitionSpec as P

BS = 64
NX = 4
NY = 4
NZ = 8
MESH = pl.DeviceIdType.MESH
ROWS = 30
STAGE = 16
HALF = 2048
QUART = 1024
WIDE = 512
ORIGINS = (0, -1, 1, 2)
CODE = 64.0
TOP = 32766.0
REACH = ((4, 3), (3, 4))


def merge(first, second):
    out = []
    for index in range(max(len(first), len(second))):
        if index < len(first):
            out.append(first[index])
        if index < len(second):
            out.append(second[index])
    return out


def kernel(
    amp_hbm, ints_hbm, cyc_hbm, dims_ref, ladder_ref, cycle_ref,
    amp_v, gat, wts, cyc_v, part, sbuf, rbuf, outf, tbl, rhs, lhs, lhs_t, cyc_p, cyc_x, cyc_s, cyc_r,
    loc_sem, ag_send, ag_recv, cc_send, cc_recv, rs_send, rs_recv, cy_send, cy_recv,
):
    blk = lax.axis_index("blk")
    z = lax.axis_index("slab")
    core = lax.rem(blk, 2)
    here = blk // 2
    x = here // NY
    y = lax.rem(here, NY)
    other = 1 - core

    amp_copy = pltpu.make_async_copy(amp_hbm, amp_v, loc_sem.at[0])
    amp_copy.start()
    wts_copies = []
    for piece in range(8):
        rows = pl.ds(piece * 512, 512)
        wts_copies.append(pltpu.make_async_copy(ints_hbm.at[rows], wts.at[rows], loc_sem.at[2 + piece]))
    cyc_copy = pltpu.make_async_copy(cyc_hbm, cyc_v, loc_sem.at[1])

    def chip(dx, dy):
        return lax.rem(x + dx + NX, NX) * NY + lax.rem(y + dy + NY, NY)

    def rel(du, dv):
        dx = (1 - core) * du + core * dv
        dy = core * du + (1 - core) * dv
        return lax.rem(x + dx + NX, NX) * NY + lax.rem(y + dy + NY, NY)

    def device(place, which):
        return (place * 2 + which, z)

    def along(step):
        return (blk, lax.rem(z + step + NZ, NZ))

    shifts = [(dx, dy) for dx in range(NX) for dy in range(NY) if (dx, dy) != (0, 0)]

    barrier = pltpu.get_barrier_semaphore()
    pl.semaphore_signal(barrier, inc=1, device_id=device(here, other), device_id_type=MESH)
    for dx, dy in shifts:
        pl.semaphore_signal(barrier, inc=1, device_id=device(chip(dx, dy), core), device_id_type=MESH)
    for step in (1, -1):
        pl.semaphore_signal(barrier, inc=1, device_id=along(step), device_id_type=MESH)

    size_c = dims_ref[z, 0]
    size_d = dims_ref[z, 1]
    amp_copy.wait()
    lane = lax.broadcasted_iota(jnp.int32, (STAGE, 2 * HALF), 1)
    valid = (lane // BS < size_c) & (lax.rem(lane, BS) < size_d)
    zero = jnp.zeros((), jnp.float32)
    for h in range(2):
        count = min(STAGE, ROWS - h * STAGE)
        mine = amp_v[h * STAGE:h * STAGE + count, :].astype(jnp.float32)
        if count < STAGE:
            mine = jnp.concatenate([mine, jnp.zeros((STAGE - count, 2 * HALF), jnp.float32)], 0)
        gat[h, pl.ds(pl.multiple_of(blk * STAGE, STAGE), STAGE), :] = jnp.where(valid, mine, zero).astype(jnp.bfloat16)

    pl.semaphore_wait(barrier, len(shifts) + 3)

    pending = []

    def send(src, dst, send_sem, recv_sem, to):
        copy = pltpu.make_async_remote_copy(
            src_ref=src, dst_ref=dst, send_sem=send_sem, recv_sem=recv_sem, device_id=to, device_id_type=MESH
        )
        copy.start()
        pending.append(copy)

    def arrived(dst, send_sem, recv_sem):
        pltpu.make_async_remote_copy(
            src_ref=dst, dst_ref=dst, send_sem=send_sem, recv_sem=recv_sem,
            device_id=device(here, other), device_id_type=MESH,
        ).wait_recv()

    def block(h, place, piece):
        rows = pl.ds(pl.multiple_of(place * 32, 32), 32)
        if piece is None:
            cols = pl.ds(pl.multiple_of(core * HALF, HALF), HALF)
        else:
            cols = pl.ds(pl.multiple_of(core * HALF + piece * QUART, QUART), QUART)
        return gat.at[h, rows, cols]

    counters = {}

    def next_of(key):
        counters[key] = counters.get(key, -1) + 1
        return counters[key]

    U_M, U_P, U2_0, U2_1 = 0, 1, 2, 3

    def slot_v(kind, origin):
        return 4 + kind * 4 + ORIGINS.index(origin)

    def push(h, place, piece, slot, to):
        ref = block(h, place, piece)
        send(ref, ref, ag_send.at[h, next_of(("ag", h))], ag_recv.at[h, slot], device(to, core))

    def got(h, place, piece, slot):
        arrived(block(h, place, piece), ag_send.at[h, 0], ag_recv.at[h, slot])

    def share(h, place):
        index = next_of(("cc", h))
        ref = block(h, place, None)
        send(ref, ref, cc_send.at[h, index], cc_recv.at[h, index], device(here, other))

    def up(h, origin, piece_place):
        push(h, piece_place, None, slot_v(0, origin), rel(0, 1))
        push(h, piece_place, None, slot_v(1, origin), rel(0, -1))

    def swap(h):
        index = next_of(("cc", h))
        ref = gat.at[h, pl.ds(pl.multiple_of(blk * STAGE, STAGE), STAGE)]
        send(ref, ref, cc_send.at[h, index], cc_recv.at[h, index], device(here, other))

    def swapped(h):
        ref = gat.at[h, pl.ds(pl.multiple_of((here * 2 + other) * STAGE, STAGE), STAGE)]
        arrived(ref, cc_send.at[h, 0], cc_recv.at[h, 0])

    def own(h):
        push(h, here, None, U_M, rel(1, 0))
        push(h, here, None, U_P, rel(-1, 0))
        up(h, 0, here)

    def first_hop(h, sign):
        place = rel(-sign, 0)
        got(h, place, None, U_M if sign > 0 else U_P)
        if sign > 0:
            push(h, place, 0, U2_0, rel(1, 0))
        else:
            push(h, place, 1, U2_1, rel(-1, 0))
        up(h, -sign, place)
        share(h, place)

    def second_hop(h):
        place = rel(2, 0)
        got(h, place, 0, U2_0)
        got(h, place, 1, U2_1)
        up(h, 2, place)
        share(h, place)

    def column_hop(h, origin):
        low = rel(origin, -1)
        got(h, low, None, slot_v(0, origin))
        push(h, low, 0, slot_v(2, origin), rel(0, 1))
        share(h, low)
        high = rel(origin, 1)
        got(h, high, None, slot_v(1, origin))
        push(h, high, 1, slot_v(3, origin), rel(0, -1))
        share(h, high)

    def column_end(h, origin):
        far = rel(origin, 2)
        got(h, far, 0, slot_v(2, origin))
        got(h, far, 1, slot_v(3, origin))
        share(h, far)

    def shared(h):
        for index in range(1, 16):
            arrived(block(h, here, None), cc_send.at[h, 0], cc_recv.at[h, index])

    def gather_steps(h):
        steps = [
            functools.partial(first_hop, h, 1),
            functools.partial(first_hop, h, -1),
            functools.partial(column_hop, h, 0),
            functools.partial(second_hop, h),
            functools.partial(column_hop, h, -1),
            functools.partial(column_hop, h, 1),
            functools.partial(column_end, h, 0),
            functools.partial(column_hop, h, 2),
        ]
        return steps

    def gather_ends(h):
        for origin in (-1, 1, 2):
            column_end(h, origin)
        shared(h)

    def product(h, half):
        def tile(n, carry):
            cols = pl.ds(pl.multiple_of(half * WIDE + n * 256, 256), 256)
            part[h, :, cols] = jnp.dot(gat[h], wts[:, cols], preferred_element_type=jnp.float32)
            return carry

        lax.fori_loop(0, 2, tile, 0)

    def chunk(h, half, dest, lb):
        rows = pl.ds(pl.multiple_of(dest * 64, 64), 64)
        return part[h, rows, half * WIDE + lb * 128:half * WIDE + (lb + 1) * 128]

    def decode(h, way, half, t):
        codes = rbuf[h, way, half, t, 256:272, :].astype(jnp.int32).astype(jnp.float32)
        scales = jnp.exp2(codes * (1.0 / CODE)) * (1.0 / TOP)
        pieces = []
        for lb in range(4):
            q = rbuf[h, way, half, t, lb * 64:(lb + 1) * 64, :].astype(jnp.int32).astype(jnp.float32)
            pieces.append(q * scales[lb:lb + 1, :])
        return pieces

    def landed(h, way, half, t):
        arrived(rbuf.at[h, way, half, t], rs_send.at[h, way, half, 0], rs_recv.at[h, way, half, t])

    def hop(h, way, half, t):
        sign = 1 if way == 0 else -1
        reach = REACH[half][way]
        if t >= reach:
            return
        dest = lax.rem(z + sign * (reach - t) + NZ, NZ)
        if t > 0:
            landed(h, way, half, t - 1)
            before = decode(h, way, half, t - 1)
        row = lax.broadcasted_iota(jnp.int32, (16, 128), 0)
        codes = jnp.zeros((16, 128), jnp.float32)
        for lb in range(4):
            v = chunk(h, half, dest, lb)
            if t > 0:
                v = v + before[lb]
            top = jnp.maximum(jnp.max(jnp.abs(v), axis=0, keepdims=True), 1e-36)
            code = jnp.ceil(jnp.log2(top) * CODE)
            q = jnp.round(v * (jnp.exp2(code * (-1.0 / CODE)) * TOP))
            sbuf[h, way, half, t, lb * 64:(lb + 1) * 64, :] = q.astype(jnp.int32).astype(jnp.int16)
            codes = jnp.where(row == lb, code, codes)
        sbuf[h, way, half, t, 256:272, :] = codes.astype(jnp.int32).astype(jnp.int16)
        send(sbuf.at[h, way, half, t], rbuf.at[h, way, half, t], rs_send.at[h, way, half, t],
             rs_recv.at[h, way, half, t], along(sign))

    def hops(h, half, t):
        hop(h, 0, half, t)
        hop(h, 1, half, t)

    q_out = blk // 4
    out_a = dims_ref[q_out, 0]
    out_b = dims_ref[q_out, 1]

    def settle(h, half):
        landed(h, 0, half, REACH[half][0] - 1)
        landed(h, 1, half, REACH[half][1] - 1)
        plus = decode(h, 0, half, REACH[half][0] - 1)
        minus = decode(h, 1, half, REACH[half][1] - 1)
        for lb in range(4):
            start = half * WIDE + lb * 128
            column = lax.broadcasted_iota(jnp.int32, (64, 128), 1) + start
            a = lax.rem(blk, 4) * 16 + column // BS
            keep = (a < out_a) & (lax.rem(column, BS) < out_b)
            total = chunk(h, half, z, lb) + plus[lb] + minus[lb]
            total = jnp.where(keep, total, 0.0)
            for g in range(4):
                count = min(STAGE, ROWS - h * STAGE)
                row0 = g * ROWS + h * STAGE
                outf[row0:row0 + count, start:start + 128] = total[g * STAGE:g * STAGE + count, :]

    def cycle_left():
        cyc_copy.wait()
        lhs[...] = jnp.zeros_like(lhs)
        for cc in range(2):
            lhs[cc * 128:cc * 128 + 120, :] = cyc_v[cc]
        lhs_t[...] = lhs[...].T

    def cycle_rows(h):
        cols = pl.ds(pl.multiple_of(blk * 128, 128), 128)
        count = min(STAGE, ROWS - h * STAGE)
        for src in range(32):
            rows = gat[h, src * STAGE:(src + 1) * STAGE, cols].astype(jnp.float32)
            tbl[src * ROWS + h * STAGE:src * ROWS + h * STAGE + count, :] = rows[:count]

    def cycle_product():
        first = lax.broadcasted_iota(jnp.int32, (120, 128), 1) < 64
        rhs[...] = jnp.zeros_like(rhs)
        for pair in range(4):
            even = tbl[pl.ds(2 * pair, 120, stride=8), :]
            odd = tbl[pl.ds(2 * pair + 1, 120, stride=8), :]
            cols = slice(pair * 128, (pair + 1) * 128)
            rhs[0:120, cols] = jnp.where(first, even, pltpu.roll(odd, 64, 1)).astype(jnp.bfloat16)
            rhs[128:248, cols] = jnp.where(first, pltpu.roll(even, 64, 1), odd).astype(jnp.bfloat16)
        for n in range(2):
            cols = slice(n * 256, (n + 1) * 256)
            term = jnp.dot(lhs_t[...], rhs[:, cols], preferred_element_type=jnp.float32)
            cyc_p[:, :, :, cols] = term.reshape(16, 2, 16, 256)
        send(cyc_p.at[:, other], cyc_x, cy_send.at[0], cy_recv.at[0], device(here, other))

    def cycle_spread():
        arrived(cyc_x, cy_send.at[0], cy_recv.at[0])
        cyc_s[...] = cyc_p[:, core] + cyc_x[...]
        for index, (dx, dy) in enumerate(shifts):
            to = chip(dx, dy)
            send(cyc_s.at[to], cyc_r.at[index], cy_send.at[1 + index], cy_recv.at[1 + index], device(to, core))

    def cycle_settle():
        total = cyc_s[here]
        for index in range(len(shifts)):
            arrived(cyc_r.at[index], cy_send.at[0], cy_recv.at[1 + index])
            total = total + cyc_r[index]
        size_a = dims_ref[z, 0]
        size_b = dims_ref[z, 1]
        a = lax.rem(blk, 4) * 16 + lax.broadcasted_iota(jnp.int32, (16, 512), 0)
        b = lax.rem(lax.broadcasted_iota(jnp.int32, (16, 512), 1), BS)
        cycle_ref[...] = jnp.where((a < size_a) & (b < size_b), total, 0.0).astype(jnp.bfloat16)

    swap(0)
    swap(1)
    swapped(0)
    own(0)
    for copy in wts_copies:
        copy.start()
    cyc_copy.start()
    for step in gather_steps(0):
        step()
    cycle_left()
    swapped(1)
    own(1)
    gather_ends(0)
    for copy in wts_copies:
        copy.wait()

    def ladder_steps(h):
        return [
            functools.partial(product, h, 0),
            functools.partial(hops, h, 0, 0),
            functools.partial(product, h, 1),
            functools.partial(hops, h, 1, 0),
            functools.partial(hops, h, 0, 1),
            functools.partial(hops, h, 1, 1),
            functools.partial(hops, h, 0, 2),
            functools.partial(hops, h, 1, 2),
            functools.partial(hops, h, 0, 3),
            functools.partial(hops, h, 1, 3),
        ]

    for step in merge(ladder_steps(0), gather_steps(1)):
        step()
    cycle_rows(0)
    gather_ends(1)
    product(1, 0)
    hops(1, 0, 0)
    product(1, 1)
    hops(1, 1, 0)
    cycle_rows(1)
    cycle_product()
    hops(1, 0, 1)
    hops(1, 1, 1)
    cycle_spread()
    settle(0, 0)
    settle(0, 1)
    hops(1, 0, 2)
    hops(1, 1, 2)
    hops(1, 0, 3)
    hops(1, 1, 3)
    cycle_settle()
    settle(1, 0)
    settle(1, 1)
    ladder_ref[...] = outf[...].astype(jnp.bfloat16)
    for copy in pending:
        copy.wait_send()


def local(amplitudes, ladder_ints, cycle_ints, block_dims):
    any_space = pl.BlockSpec(memory_space=pl.ANY)
    vmem = pl.BlockSpec(memory_space=pltpu.VMEM)
    dma = pltpu.SemaphoreType.DMA
    ladder, cycle = pl.pallas_call(
        kernel,
        out_shape=(
            jax.ShapeDtypeStruct((120, 1024), jnp.bfloat16),
            jax.ShapeDtypeStruct((16, 512), jnp.bfloat16),
        ),
        in_specs=[any_space, any_space, any_space, pl.BlockSpec(memory_space=pltpu.SMEM)],
        out_specs=(vmem, vmem),
        scratch_shapes=[
            pltpu.VMEM((ROWS, 2 * HALF), jnp.bfloat16),
            pltpu.VMEM((2, 512, 4096), jnp.bfloat16),
            pltpu.VMEM((4096, 1024), jnp.bfloat16),
            pltpu.VMEM((2, 120, 512), jnp.bfloat16),
            pltpu.VMEM((2, 512, 1024), jnp.float32),
            pltpu.VMEM((2, 2, 2, 4, 272, 128), jnp.int16),
            pltpu.VMEM((2, 2, 2, 4, 272, 128), jnp.int16),
            pltpu.VMEM((120, 1024), jnp.float32),
            pltpu.VMEM((960, 128), jnp.float32),
            pltpu.VMEM((256, 512), jnp.bfloat16),
            pltpu.VMEM((256, 512), jnp.bfloat16),
            pltpu.VMEM((512, 256), jnp.bfloat16),
            pltpu.VMEM((16, 2, 16, 512), jnp.float32),
            pltpu.VMEM((16, 16, 512), jnp.float32),
            pltpu.VMEM((16, 16, 512), jnp.float32),
            pltpu.VMEM((15, 16, 512), jnp.float32),
            dma((10,)),
            dma((2, 20)),
            dma((2, 20)),
            dma((2, 16)),
            dma((2, 16)),
            dma((2, 2, 2, 4)),
            dma((2, 2, 2, 4)),
            dma((16,)),
            dma((16,)),
        ],
        compiler_params=pltpu.CompilerParams(
            collective_id=0, has_side_effects=True, vmem_limit_bytes=56 << 20
        ),
    )(amplitudes, ladder_ints, cycle_ints[0], block_dims)
    return ladder, cycle[None]


def solution(mesh):
    in_specs = (P("blk", "slab"), P("slab", "blk"), P("slab", "blk", None, None), P())
    out_specs = (P("slab", "blk"), P("slab", "blk", None))
    return jax.shard_map(local, mesh=mesh, in_specs=in_specs, out_specs=out_specs, check_vma=False)
```

time: 234 us -> 76 us (0.32); the launches traced: 230 us -> 74.9 us
  waiting for transfers between devices: 181 us -> 0 us
  Pallas kernels: 0 us -> 70 us
  matrix products: 14.6 us -> 0 us
  between operations: 13.8 us -> 0.64 us
  local copies, waits for them, and re-layouts: 12.8 us -> 4.32 us
  other arithmetic: 7.16 us -> 0 us
    reduce_scatter x2 -> x0, waiting for transfers between devices: 120 us -> none  [the longest x1 68.4 us: local(): lax.psum_scatter(cycle_term, 'blk', scatter_dimension=0, tiled=True)]
    pallas_call x0 -> x1, Pallas kernels: none -> 70 us  [local(): pl.pallas_call(kernel, out_shape=(jax.ShapeDtypeStruct((120, 1024), jnp.b...]
    all_gather x1 -> x0, waiting for transfers between devices: 61.1 us -> none  [local(): gathered = lax.all_gather(masked, 'blk', axis=0, tiled=True)]
    dot_general x2 -> x0, matrix products: 14.6 us -> none  [the longest x1 14.3 us: local(): jnp.dot(gathered, ladder_ints, preferred_element_type=jnp.float32)]
    unnamed x5 -> x3, local copies, waits for them, and re-layouts: 9.55 us -> 4.32 us
  transfers between devices with their start and end apart: 3 -> 0, of which waited for: 3 -> 0; matrix products, arithmetic and copies ran while one was open for 8% -> 0% of each run, Pallas kernels for 0% -> 0%
where the time goes in v2:
time: 76 us; the launch traced here: 74.9 us
  Pallas kernels  70 us (92%)
  local copies, waits for them, and re-layouts  4.32 us (6%)
    pallas_call x1, Pallas kernels, local(): pl.pallas_call(kernel, out_shape=(jax.ShapeDtypeStruct((120, 1024), jnp.b...  70 us
    unnamed x3, local copies, waits for them, and re-layouts  4.32 us

profile of v2, /device:TPU:32, one launch (start us, length us, event | category | flops | bytes accessed | tf_op | source)
XLA Modules:
  0.0 74.9 jit_solution(18387900617084271212)
XLA Ops:
  0.6 1.3 %copy.6.dims_ref = s32[8,2]{1,0:T(8,128)} copy(s32[8,2]{0,1:T(2,128)} %param.7) | data formatting | bytes 128 | tf_op args[3]
  2.0 70.0 %shard_map.59 = (bf16[120,1024]{1,0:T(8,128)(2,1)}, bf16[16,512]{1,0:T(8,128)(2,1)}) custom-call(bf16[30,4096]{1,0:T(8,128)(2,1)} %amp_hbm.1, bf16[4096,1024]{1,0:T(8,128)(2,1)} %ints_hbm.1, bf16[2,120,512]{2,1,0:T(8,128)(2,1)} %bitcast.2, s32[8,2]{1,0:T(8,128)} %copy.6.dims_ref), custom_call_target="tpu_custom_call" | custom-call | tf_op jit(solution)/shard_map/pallas_call | solution.py:395
  72.0 1.7 %copy.9 = bf16[120,1024]{1,0:T(8,128)(2,1)} copy(bf16[120,1024]{1,0:T(8,128)(2,1)} %get-tuple-element.8) | data formatting | bytes 491520
  73.6 1.3 %copy.10 = bf16[1,16,512]{2,1,0:T(8,128)(2,1)} copy(bf16[1,16,512]{2,1,0:T(8,128)(2,1)} %bitcast.3) | data formatting | bytes 32768

commit v3 on v2

v3 whole, which is shorter than its diff:
```python
import jax
import jax.numpy as jnp
from jax import lax
from jax.experimental import pallas as pl
from jax.experimental.pallas import tpu as pltpu
from jax.sharding import PartitionSpec as P

BS = 64
NX = 4
NY = 4
NZ = 8
MESH = pl.DeviceIdType.MESH
ROWS = 30
STAGE = 8
STAGES = 4
BLOCK = 16
CHUNK = 32
HALF = 2048
QUART = 1024
WIDE = 512
STRAIGHT = (0, 3)
ORIGINS = (0, -1, 1, 2)
CODE = 64.0
TOP = 32766.0
REACH = ((4, 3), (3, 4))


def kernel(
    amp_hbm, ints_hbm, cyc_hbm, dims_ref, ladder_ref, cycle_ref,
    amp_v, mine_v, their_v, gat, wts, cyc_v, part, sbuf, rbuf, outf, tbl, rhs, lhs, lhs_t, cyc_p, cyc_x, cyc_s, cyc_r,
    loc_sem, sw_send, sw_recv, ag_send, ag_recv, cc_send, cc_recv, rs_send, rs_recv, cy_send, cy_recv,
):
    blk = lax.axis_index("blk")
    z = lax.axis_index("slab")
    core = lax.rem(blk, 2)
    here = blk // 2
    x = here // NY
    y = lax.rem(here, NY)
    other = 1 - core

    amp_copy = pltpu.make_async_copy(amp_hbm, amp_v, loc_sem.at[0])
    amp_copy.start()
    wts_copies = []
    for piece in range(8):
        rows = pl.ds(piece * 512, 512)
        wts_copies.append(pltpu.make_async_copy(ints_hbm.at[rows], wts.at[rows], loc_sem.at[2 + piece]))
    cyc_copy = pltpu.make_async_copy(cyc_hbm, cyc_v, loc_sem.at[1])
    for copy in wts_copies:
        copy.start()
    cyc_copy.start()

    def chip(dx, dy):
        return lax.rem(x + dx + NX, NX) * NY + lax.rem(y + dy + NY, NY)

    def rel(du, dv):
        dx = (1 - core) * du + core * dv
        dy = core * du + (1 - core) * dv
        return lax.rem(x + dx + NX, NX) * NY + lax.rem(y + dy + NY, NY)

    def device(place, which):
        return (place * 2 + which, z)

    def along(step):
        return (blk, lax.rem(z + step + NZ, NZ))

    shifts = [(dx, dy) for dx in range(NX) for dy in range(NY) if (dx, dy) != (0, 0)]

    barrier = pltpu.get_barrier_semaphore()
    pl.semaphore_signal(barrier, inc=1, device_id=device(here, other), device_id_type=MESH)
    for dx, dy in shifts:
        pl.semaphore_signal(barrier, inc=1, device_id=device(chip(dx, dy), core), device_id_type=MESH)
    for step in (1, -1):
        pl.semaphore_signal(barrier, inc=1, device_id=along(step), device_id_type=MESH)

    size_c = dims_ref[0, z]
    size_d = dims_ref[1, z]
    amp_copy.wait()
    lane = lax.broadcasted_iota(jnp.int32, (ROWS, 2 * HALF), 1)
    valid = (lane // BS < size_c) & (lax.rem(lane, BS) < size_d)
    masked = jnp.where(valid, amp_v[...].astype(jnp.float32), 0.0).astype(jnp.bfloat16)
    mine_v[STAGE * STAGES - BLOCK:, :] = jnp.zeros((BLOCK, 2 * HALF), jnp.bfloat16)
    mine_v[0:ROWS, :] = masked

    pl.semaphore_wait(barrier, len(shifts) + 3)

    pending = []

    def send(src, dst, send_sem, recv_sem, to):
        copy = pltpu.make_async_remote_copy(
            src_ref=src, dst_ref=dst, send_sem=send_sem, recv_sem=recv_sem, device_id=to, device_id_type=MESH
        )
        copy.start()
        pending.append(copy)

    def arrived(dst, send_sem, recv_sem):
        pltpu.make_async_remote_copy(
            src_ref=dst, dst_ref=dst, send_sem=send_sem, recv_sem=recv_sem,
            device_id=device(here, other), device_id_type=MESH,
        ).wait_recv()

    def block(h, place, piece):
        rows = pl.ds(pl.multiple_of(place * BLOCK, BLOCK), BLOCK)
        if piece is None:
            cols = pl.ds(pl.multiple_of(core * HALF, HALF), HALF)
        else:
            cols = pl.ds(pl.multiple_of(core * HALF + piece * QUART, QUART), QUART)
        return gat.at[h, rows, cols]

    counters = {}

    def next_of(key):
        counters[key] = counters.get(key, -1) + 1
        return counters[key]

    U_M, U_P, U2_0, U2_1 = 0, 1, 2, 3

    def slot_v(kind, origin):
        return 4 + kind * 4 + ORIGINS.index(origin)

    def push(h, place, piece, slot, to):
        ref = block(h, place, piece)
        send(ref, ref, ag_send.at[h, next_of(("ag", h))], ag_recv.at[h, slot], device(to, core))

    def got(h, place, piece, slot):
        arrived(block(h, place, piece), ag_send.at[h, 0], ag_recv.at[h, slot])

    def share(h, place):
        index = next_of(("cc", h))
        ref = block(h, place, None)
        send(ref, ref, cc_send.at[h, index], cc_recv.at[h, index], device(here, other))

    def up(h, origin, piece_place):
        push(h, piece_place, None, slot_v(0, origin), rel(0, 1))
        push(h, piece_place, None, slot_v(1, origin), rel(0, -1))

    def swap(part_of):
        rows = pl.ds(part_of * BLOCK, BLOCK)
        send(mine_v.at[rows], their_v.at[rows], sw_send.at[part_of], sw_recv.at[part_of], device(here, other))

    def swapped(part_of):
        rows = pl.ds(part_of * BLOCK, BLOCK)
        arrived(their_v.at[rows], sw_send.at[part_of], sw_recv.at[part_of])

    def assemble(h):
        pair = slice(h // 2 * BLOCK, h // 2 * BLOCK + BLOCK)
        start = h % 2 * STAGE
        mine = mine_v[pair, :].astype(jnp.float32)[start:start + STAGE]
        theirs = their_v[pair, :].astype(jnp.float32)[start:start + STAGE]
        low = jnp.where(core == 0, mine, theirs)
        high = jnp.where(core == 0, theirs, mine)
        gat[h, pl.ds(pl.multiple_of(here * BLOCK, BLOCK), BLOCK), :] = jnp.concatenate([low, high], 0).astype(jnp.bfloat16)

    def own(h):
        push(h, here, None, U_M, rel(1, 0))
        push(h, here, None, U_P, rel(-1, 0))
        if h in STRAIGHT:
            push(h, here, None, U2_0, rel(2, 0))
        up(h, 0, here)

    def first_hop(h, sign):
        place = rel(-sign, 0)
        got(h, place, None, U_M if sign > 0 else U_P)
        if h in STRAIGHT:
            pass
        elif sign > 0:
            push(h, place, 0, U2_0, rel(1, 0))
        else:
            push(h, place, 1, U2_1, rel(-1, 0))
        up(h, -sign, place)
        share(h, place)

    def second_hop(h):
        place = rel(2, 0)
        if h in STRAIGHT:
            got(h, place, None, U2_0)
        else:
            got(h, place, 0, U2_0)
            got(h, place, 1, U2_1)
        up(h, 2, place)
        share(h, place)

    def column_low(h, origin):
        low = rel(origin, -1)
        got(h, low, None, slot_v(0, origin))
        push(h, low, 0, slot_v(2, origin), rel(0, 1))
        share(h, low)

    def column_high(h, origin):
        high = rel(origin, 1)
        got(h, high, None, slot_v(1, origin))
        push(h, high, 1, slot_v(3, origin), rel(0, -1))
        share(h, high)

    def column_end(h, origin):
        far = rel(origin, 2)
        got(h, far, 0, slot_v(2, origin))
        got(h, far, 1, slot_v(3, origin))
        share(h, far)

    def shared(h):
        for index in range(15):
            arrived(block(h, here, None), cc_send.at[h, 0], cc_recv.at[h, index])

    def product(h, half):
        cols = slice(half * WIDE, (half + 1) * WIDE)
        part[h, :, cols] = jnp.dot(gat[h], wts[:, cols], preferred_element_type=jnp.float32)

    def chunk(h, half, dest, lb):
        rows = pl.ds(pl.multiple_of(dest * CHUNK, CHUNK), CHUNK)
        return part[h, rows, half * WIDE + lb * 128:half * WIDE + (lb + 1) * 128]

    def decode(h, way, half, t):
        codes = rbuf[h, way, half, t, 4 * CHUNK:, :].astype(jnp.int32).astype(jnp.float32)
        scales = jnp.exp2(codes * (1.0 / CODE)) * (1.0 / TOP)
        pieces = []
        for lb in range(4):
            q = rbuf[h, way, half, t, lb * CHUNK:(lb + 1) * CHUNK, :].astype(jnp.int32).astype(jnp.float32)
            pieces.append(q * scales[lb:lb + 1, :])
        return pieces

    def landed(h, way, half, t):
        arrived(rbuf.at[h, way, half, t], rs_send.at[h, way, half, 0], rs_recv.at[h, way, half, t])

    def hop(h, way, half, t):
        sign = 1 if way == 0 else -1
        reach = REACH[half][way]
        if t >= reach:
            return
        dest = lax.rem(z + sign * (reach - t) + NZ, NZ)
        if t > 0:
            landed(h, way, half, t - 1)
            before = decode(h, way, half, t - 1)
        row = lax.broadcasted_iota(jnp.int32, (8, 128), 0)
        codes = jnp.zeros((8, 128), jnp.float32)
        for lb in range(4):
            v = chunk(h, half, dest, lb)
            if t > 0:
                v = v + before[lb]
            top = jnp.maximum(jnp.max(jnp.abs(v), axis=0, keepdims=True), 1e-36)
            code = jnp.ceil(jnp.log2(top) * CODE)
            q = jnp.round(v * (jnp.exp2(code * (-1.0 / CODE)) * TOP))
            sbuf[h, way, half, t, lb * CHUNK:(lb + 1) * CHUNK, :] = q.astype(jnp.int32).astype(jnp.int16)
            codes = jnp.where(row == lb, code, codes)
        sbuf[h, way, half, t, 4 * CHUNK:, :] = codes.astype(jnp.int32).astype(jnp.int16)
        send(sbuf.at[h, way, half, t], rbuf.at[h, way, half, t], rs_send.at[h, way, half, t],
             rs_recv.at[h, way, half, t], along(sign))

    def hops(h, half, t):
        hop(h, 0, half, t)
        hop(h, 1, half, t)

    q_out = blk // 4
    out_a = dims_ref[0, q_out]
    out_b = dims_ref[1, q_out]

    def settle(h, half):
        landed(h, 0, half, REACH[half][0] - 1)
        landed(h, 1, half, REACH[half][1] - 1)
        plus = decode(h, 0, half, REACH[half][0] - 1)
        minus = decode(h, 1, half, REACH[half][1] - 1)
        for lb in range(4):
            start = half * WIDE + lb * 128
            column = lax.broadcasted_iota(jnp.int32, (CHUNK, 128), 1) + start
            a = lax.rem(blk, 4) * 16 + column // BS
            keep = (a < out_a) & (lax.rem(column, BS) < out_b)
            total = chunk(h, half, z, lb) + plus[lb] + minus[lb]
            total = jnp.where(keep, total, 0.0)
            count = min(STAGE, ROWS - h * STAGE)
            for g in range(4):
                row0 = g * ROWS + h * STAGE
                outf[row0:row0 + count, start:start + 128] = total[g * STAGE:g * STAGE + count, :]

    def cycle_left():
        cyc_copy.wait()
        lhs[...] = jnp.zeros_like(lhs)
        for cc in range(2):
            lhs[cc * 128:cc * 128 + 120, :] = cyc_v[cc]
        lhs_t[...] = lhs[...].T

    def cycle_rows(h):
        cols = pl.ds(pl.multiple_of(blk * 128, 128), 128)
        count = min(STAGE, ROWS - h * STAGE)
        rows = gat[h, :, cols].astype(jnp.float32)
        for src in range(32):
            tbl[src * ROWS + h * STAGE:src * ROWS + h * STAGE + count, :] = rows[src * STAGE:src * STAGE + count]

    def cycle_product():
        first = lax.broadcasted_iota(jnp.int32, (120, 128), 1) < 64
        rhs[...] = jnp.zeros_like(rhs)
        for pair in range(4):
            even = tbl[pl.ds(2 * pair, 120, stride=8), :]
            odd = tbl[pl.ds(2 * pair + 1, 120, stride=8), :]
            cols = slice(pair * 128, (pair + 1) * 128)
            rhs[0:120, cols] = jnp.where(first, even, pltpu.roll(odd, 64, 1)).astype(jnp.bfloat16)
            rhs[128:248, cols] = jnp.where(first, pltpu.roll(even, 64, 1), odd).astype(jnp.bfloat16)
        for n in range(2):
            cols = slice(n * 256, (n + 1) * 256)
            term = jnp.dot(lhs_t[...], rhs[:, cols], preferred_element_type=jnp.float32)
            cyc_p[:, :, :, cols] = term.reshape(16, 2, 16, 256)
        send(cyc_p.at[:, other], cyc_x, cy_send.at[0], cy_recv.at[0], device(here, other))

    def cycle_spread():
        arrived(cyc_x, cy_send.at[0], cy_recv.at[0])
        cyc_s[...] = cyc_p[:, core] + cyc_x[...]
        for index, (dx, dy) in enumerate(shifts):
            to = chip(dx, dy)
            send(cyc_s.at[to], cyc_r.at[index], cy_send.at[1 + index], cy_recv.at[1 + index], device(to, core))

    def cycle_settle():
        total = cyc_s[here]
        for index in range(len(shifts)):
            arrived(cyc_r.at[index], cy_send.at[0], cy_recv.at[1 + index])
            total = total + cyc_r[index]
        size_a = dims_ref[0, z]
        size_b = dims_ref[1, z]
        a = lax.rem(blk, 4) * 16 + lax.broadcasted_iota(jnp.int32, (16, 512), 0)
        b = lax.rem(lax.broadcasted_iota(jnp.int32, (16, 512), 1), BS)
        cycle_ref[...] = jnp.where((a < size_a) & (b < size_b), total, 0.0).astype(jnp.bfloat16)

    swap(0)
    swap(1)
    swapped(0)
    assemble(0)
    own(0)
    assemble(1)
    swapped(1)
    for h in range(2, STAGES):
        assemble(h)
    own(1)
    first_hop(0, 1)
    first_hop(0, -1)
    column_low(0, 0)
    column_high(0, 0)
    second_hop(0)
    first_hop(1, 1)
    column_low(1, 0)
    first_hop(1, -1)
    column_high(1, 0)
    column_low(0, -1)
    column_high(0, -1)
    column_low(0, 1)
    column_high(0, 1)
    column_end(0, 0)
    column_high(0, 2)
    column_low(0, 2)
    second_hop(1)
    column_low(1, -1)
    column_high(1, -1)
    own(2)
    column_high(1, 1)
    column_low(1, 1)
    column_end(1, 0)
    column_end(0, -1)
    column_end(0, 1)
    column_end(0, 2)
    own(3)
    column_low(1, 2)
    column_high(1, 2)
    shared(0)
    for copy in wts_copies:
        copy.wait()
    cycle_left()
    product(0, 0)
    hops(0, 0, 0)
    column_end(1, -1)
    first_hop(2, 1)
    column_end(1, 1)
    first_hop(2, -1)
    column_low(2, 0)
    column_high(2, 0)
    first_hop(3, 1)
    first_hop(3, -1)
    product(0, 1)
    hops(0, 1, 0)
    column_end(1, 2)
    column_low(3, 0)
    column_high(3, 0)
    second_hop(3)
    cycle_rows(0)
    hops(0, 0, 1)
    second_hop(2)
    column_low(2, -1)
    column_high(2, -1)
    shared(1)
    column_low(2, 1)
    column_high(2, 1)
    product(1, 0)
    hops(0, 1, 1)
    hops(1, 0, 0)
    column_end(2, 0)
    column_low(3, -1)
    column_high(3, -1)
    column_low(3, 1)
    column_high(3, 1)
    hops(0, 0, 2)
    column_end(3, 0)
    column_low(3, 2)
    column_high(3, 2)
    product(1, 1)
    hops(1, 1, 0)
    column_low(2, 2)
    column_high(2, 2)
    column_end(2, -1)
    column_end(2, 1)
    hops(0, 1, 2)
    column_end(3, -1)
    cycle_rows(1)
    column_end(3, 1)
    hops(1, 0, 1)
    column_end(3, 2)
    hops(0, 0, 3)
    shared(3)
    column_end(2, 2)
    hops(1, 1, 1)
    product(3, 0)
    hops(0, 1, 3)
    hops(1, 0, 2)
    hops(3, 0, 0)
    product(3, 1)
    hops(3, 1, 0)
    shared(2)
    hops(1, 1, 2)
    product(2, 0)
    hops(1, 0, 3)
    hops(2, 0, 0)
    product(2, 1)
    hops(2, 1, 0)
    hops(3, 0, 1)
    hops(3, 1, 1)
    settle(0, 0)
    settle(0, 1)
    cycle_rows(2)
    hops(1, 1, 3)
    cycle_rows(3)
    cycle_product()
    hops(2, 0, 1)
    settle(1, 0)
    hops(2, 1, 1)
    hops(3, 0, 2)
    hops(3, 1, 2)
    cycle_spread()
    settle(1, 1)
    hops(2, 0, 2)
    hops(2, 1, 2)
    hops(3, 0, 3)
    hops(3, 1, 3)
    hops(2, 0, 3)
    hops(2, 1, 3)
    cycle_settle()
    settle(3, 0)
    settle(3, 1)
    settle(2, 0)
    settle(2, 1)
    ladder_ref[...] = outf[...].astype(jnp.bfloat16)
    for copy in pending:
        copy.wait_send()


def local(amplitudes, ladder_ints, cycle_ints, block_dims):
    any_space = pl.BlockSpec(memory_space=pl.ANY)
    vmem = pl.BlockSpec(memory_space=pltpu.VMEM)
    dma = pltpu.SemaphoreType.DMA
    ladder, cycle = pl.pallas_call(
        kernel,
        out_shape=(
            jax.ShapeDtypeStruct((120, 1024), jnp.bfloat16),
            jax.ShapeDtypeStruct((16, 512), jnp.bfloat16),
        ),
        in_specs=[any_space, any_space, any_space, pl.BlockSpec(memory_space=pltpu.SMEM)],
        out_specs=(vmem, vmem),
        scratch_shapes=[
            pltpu.VMEM((ROWS, 2 * HALF), jnp.bfloat16),
            pltpu.VMEM((STAGE * STAGES, 2 * HALF), jnp.bfloat16),
            pltpu.VMEM((STAGE * STAGES, 2 * HALF), jnp.bfloat16),
            pltpu.VMEM((STAGES, 256, 4096), jnp.bfloat16),
            pltpu.VMEM((4096, 1024), jnp.bfloat16),
            pltpu.VMEM((2, 120, 512), jnp.bfloat16),
            pltpu.VMEM((STAGES, 256, 1024), jnp.float32),
            pltpu.VMEM((STAGES, 2, 2, 4, 4 * CHUNK + 8, 128), jnp.int16),
            pltpu.VMEM((STAGES, 2, 2, 4, 4 * CHUNK + 8, 128), jnp.int16),
            pltpu.VMEM((120, 1024), jnp.float32),
            pltpu.VMEM((960, 128), jnp.float32),
            pltpu.VMEM((256, 512), jnp.bfloat16),
            pltpu.VMEM((256, 512), jnp.bfloat16),
            pltpu.VMEM((512, 256), jnp.bfloat16),
            pltpu.VMEM((16, 2, 16, 512), jnp.float32),
            pltpu.VMEM((16, 16, 512), jnp.float32),
            pltpu.VMEM((16, 16, 512), jnp.float32),
            pltpu.VMEM((15, 16, 512), jnp.float32),
            dma((10,)),
            dma((2,)),
            dma((2,)),
            dma((STAGES, 20)),
            dma((STAGES, 20)),
            dma((STAGES, 15)),
            dma((STAGES, 15)),
            dma((STAGES, 2, 2, 4)),
            dma((STAGES, 2, 2, 4)),
            dma((16,)),
            dma((16,)),
        ],
        compiler_params=pltpu.CompilerParams(
            collective_id=0, has_side_effects=True, vmem_limit_bytes=56 << 20
        ),
    )(amplitudes, ladder_ints, cycle_ints[0], block_dims.T)
    def hand_over(ladder_in, cycle_in, ladder_out, cycle_out):
        ladder_out[...] = ladder_in[...]
        cycle_out[...] = cycle_in[...]

    ladder, cycle = pl.pallas_call(
        hand_over,
        out_shape=(
            jax.ShapeDtypeStruct((120, 1024), jnp.bfloat16),
            jax.ShapeDtypeStruct((16, 512), jnp.bfloat16),
        ),
        in_specs=[vmem, vmem],
        out_specs=(vmem, vmem),
    )(ladder, cycle)
    return ladder, cycle[None]


def solution(mesh):
    in_specs = (P("blk", "slab"), P("slab", "blk"), P("slab", "blk", None, None), P())
    out_specs = (P("slab", "blk"), P("slab", "blk", None))
    return jax.shard_map(local, mesh=mesh, in_specs=in_specs, out_specs=out_specs, check_vma=False)
```

time: 76 us -> 65.9 us (0.87); the launches traced: 74.9 us -> 65.7 us
  Pallas kernels: 70 us -> 65.1 us
  local copies, waits for them, and re-layouts: 4.32 us -> 0 us
    pallas_call x1, Pallas kernels: 70 us -> 63.4 us  [local(): pl.pallas_call(kernel, out_shape=(jax.ShapeDtypeStruct((120, 1024), jnp.b...]
    unnamed x3 -> x0, local copies, waits for them, and re-layouts: 4.32 us -> none
    pallas_call x0 -> x1, Pallas kernels: none -> 1.66 us  [local(): pl.pallas_call(hand_over, out_shape=(jax.ShapeDtypeStruct((120, 1024), jn...]
where the time goes in v3:
time: 65.9 us; the launch traced here: 65.7 us
  Pallas kernels  65.1 us (99%)
    pallas_call x1, Pallas kernels, local(): pl.pallas_call(kernel, out_shape=(jax.ShapeDtypeStruct((120, 1024), jnp.b...  63.4 us
    pallas_call x1, Pallas kernels, local(): pl.pallas_call(hand_over, out_shape=(jax.ShapeDtypeStruct((120, 1024), jn...  1.66 us

profile of v3, /device:TPU:32, one launch (start us, length us, event | category | flops | bytes accessed | tf_op | source)
XLA Modules:
  0.0 65.7 jit_solution(6521696685823071959)
XLA Ops:
  0.6 63.4 %shard_map.59 = (bf16[120,1024]{1,0:T(8,128)(2,1)}, bf16[16,512]{1,0:T(8,128)(2,1)}) custom-call(bf16[30,4096]{1,0:T(8,128)(2,1)} %amp_hbm.1, bf16[4096,1024]{1,0:T(8,128)(2,1)} %ints_hbm.1, bf16[2,120,512]{2,1,0:T(8,128)(2,1)} %bitcast.3, s32[2,8]{1,0:T(2,128)} %bitcast.4), custom_call_target="tpu_custom_call" | custom-call | tf_op jit(solution)/shard_map/pallas_call | solution.py:463
  64.0 1.7 %shard_map.60 = (bf16[120,1024]{1,0:T(8,128)(2,1)}, bf16[16,512]{1,0:T(8,128)(2,1)}) custom-call(bf16[120,1024]{1,0:T(8,128)(2,1)} %get-tuple-element.6.ladder_in, bf16[16,512]{1,0:T(8,128)(2,1)} %get-tuple-element.7.cycle_in), custom_call_target="tpu_custom_call" | custom-call | tf_op jit(solution)/shard_map/pallas_call | solution.py:510

commit v4 on v3

--- a/solution.py
+++ b/solution.py
@@ -18,7 +18,8 @@
 HALF = 2048
 QUART = 1024
 WIDE = 512
-STRAIGHT = (0, 3)
+STRAIGHT = (0, 2)
+FAST = (0, 1, 3)
 ORIGINS = (0, -1, 1, 2)
 CODE = 64.0
 TOP = 32766.0
@@ -26,8 +27,8 @@
 
 
 def kernel(
-    amp_hbm, ints_hbm, cyc_hbm, dims_ref, ladder_ref, cycle_ref,
-    amp_v, mine_v, their_v, gat, wts, cyc_v, part, sbuf, rbuf, outf, tbl, rhs, lhs, lhs_t, cyc_p, cyc_x, cyc_s, cyc_r,
+    amp_hbm, ints_hbm, cyc_hbm, dims_hbm, ladder_ref, cycle_ref,
+    dims_ref, amp_v, mine_v, their_v, gat, wts, cyc_v, part, sbuf, rbuf, outf, tbl, rhs, lhs, lhs_t, cyc_p, cyc_x, cyc_s, cyc_r,
     loc_sem, sw_send, sw_recv, ag_send, ag_recv, cc_send, cc_recv, rs_send, rs_recv, cy_send, cy_recv,
 ):
     blk = lax.axis_index("blk")
@@ -40,6 +41,8 @@
 
     amp_copy = pltpu.make_async_copy(amp_hbm, amp_v, loc_sem.at[0])
     amp_copy.start()
+    dims_copy = pltpu.make_async_copy(dims_hbm, dims_ref, loc_sem.at[10])
+    dims_copy.start()
     wts_copies = []
     for piece in range(8):
         rows = pl.ds(piece * 512, 512)
@@ -69,9 +72,10 @@
     pl.semaphore_signal(barrier, inc=1, device_id=device(here, other), device_id_type=MESH)
     for dx, dy in shifts:
         pl.semaphore_signal(barrier, inc=1, device_id=device(chip(dx, dy), core), device_id_type=MESH)
-    for step in (1, -1):
+    for step in (1, -1, 2, -2):
         pl.semaphore_signal(barrier, inc=1, device_id=along(step), device_id_type=MESH)
 
+    dims_copy.wait()
     size_c = dims_ref[0, z]
     size_d = dims_ref[1, z]
     amp_copy.wait()
@@ -81,7 +85,7 @@
     mine_v[STAGE * STAGES - BLOCK:, :] = jnp.zeros((BLOCK, 2 * HALF), jnp.bfloat16)
     mine_v[0:ROWS, :] = masked
 
-    pl.semaphore_wait(barrier, len(shifts) + 3)
+    pl.semaphore_wait(barrier, len(shifts) + 5)
 
     pending = []
 
@@ -221,33 +225,49 @@
     def landed(h, way, half, t):
         arrived(rbuf.at[h, way, half, t], rs_send.at[h, way, half, 0], rs_recv.at[h, way, half, t])
 
-    def hop(h, way, half, t):
+    def emit(h, way, half, slot, ahead, earlier, far):
         sign = 1 if way == 0 else -1
-        reach = REACH[half][way]
-        if t >= reach:
-            return
-        dest = lax.rem(z + sign * (reach - t) + NZ, NZ)
-        if t > 0:
-            landed(h, way, half, t - 1)
-            before = decode(h, way, half, t - 1)
+        dest = lax.rem(z + sign * ahead + NZ, NZ)
+        before = []
+        for known in earlier:
+            landed(h, way, half, known)
+            before.append(decode(h, way, half, known))
         row = lax.broadcasted_iota(jnp.int32, (8, 128), 0)
         codes = jnp.zeros((8, 128), jnp.float32)
         for lb in range(4):
             v = chunk(h, half, dest, lb)
-            if t > 0:
-                v = v + before[lb]
+            for pieces in before:
+                v = v + pieces[lb]
             top = jnp.maximum(jnp.max(jnp.abs(v), axis=0, keepdims=True), 1e-36)
             code = jnp.ceil(jnp.log2(top) * CODE)
             q = jnp.round(v * (jnp.exp2(code * (-1.0 / CODE)) * TOP))
-            sbuf[h, way, half, t, lb * CHUNK:(lb + 1) * CHUNK, :] = q.astype(jnp.int32).astype(jnp.int16)
+            sbuf[h, way, half, slot, lb * CHUNK:(lb + 1) * CHUNK, :] = q.astype(jnp.int32).astype(jnp.int16)
             codes = jnp.where(row == lb, code, codes)
-        sbuf[h, way, half, t, 4 * CHUNK:, :] = codes.astype(jnp.int32).astype(jnp.int16)
-        send(sbuf.at[h, way, half, t], rbuf.at[h, way, half, t], rs_send.at[h, way, half, t],
-             rs_recv.at[h, way, half, t], along(sign))
+        sbuf[h, way, half, slot, 4 * CHUNK:, :] = codes.astype(jnp.int32).astype(jnp.int16)
+        send(sbuf.at[h, way, half, slot], rbuf.at[h, way, half, slot], rs_send.at[h, way, half, slot],
+             rs_recv.at[h, way, half, slot], along(sign * far))
+
+    def hop(h, way, half, t):
+        reach = REACH[half][way]
+        if t < reach:
+            emit(h, way, half, t, reach - t, [t - 1] if t > 0 else [], 1)
 
     def hops(h, half, t):
-        hop(h, 0, half, t)
-        hop(h, 1, half, t)
+        if h not in FAST:
+            hop(h, 0, half, t)
+            hop(h, 1, half, t)
+            return
+        long = 0 if REACH[half][0] == 4 else 1
+        if t == 0:
+            emit(h, long, half, 0, 4, [], 1)
+            hop(h, 1 - long, half, 0)
+            emit(h, long, half, 1, 2, [], 1)
+        elif t == 1:
+            emit(h, long, half, 2, 3, [0], 2)
+            hop(h, 1 - long, half, 1)
+        elif t == 2:
+            emit(h, long, half, 3, 1, [1, 2], 1)
+            hop(h, 1 - long, half, 2)
 
     q_out = blk // 4
     out_a = dims_ref[0, q_out]
@@ -332,10 +352,10 @@
     column_low(0, 0)
     column_high(0, 0)
     second_hop(0)
+    column_low(1, 0)
+    column_high(1, 0)
     first_hop(1, 1)
-    column_low(1, 0)
     first_hop(1, -1)
-    column_high(1, 0)
     column_low(0, -1)
     column_high(0, -1)
     column_low(0, 1)
@@ -343,113 +363,107 @@
     column_end(0, 0)
     column_high(0, 2)
     column_low(0, 2)
+    own(2)
     second_hop(1)
+    column_end(1, 0)
     column_low(1, -1)
     column_high(1, -1)
-    own(2)
+    column_low(1, 1)
     column_high(1, 1)
-    column_low(1, 1)
-    column_end(1, 0)
+    own(3)
     column_end(0, -1)
     column_end(0, 1)
     column_end(0, 2)
-    own(3)
-    column_low(1, 2)
-    column_high(1, 2)
+    first_hop(2, 1)
+    first_hop(2, -1)
     shared(0)
+    column_low(2, 0)
+    column_high(2, 0)
     for copy in wts_copies:
         copy.wait()
     cycle_left()
     product(0, 0)
     hops(0, 0, 0)
+    column_low(1, 2)
+    column_high(1, 2)
     column_end(1, -1)
-    first_hop(2, 1)
+    second_hop(2)
     column_end(1, 1)
-    first_hop(2, -1)
-    column_low(2, 0)
-    column_high(2, 0)
     first_hop(3, 1)
     first_hop(3, -1)
     product(0, 1)
     hops(0, 1, 0)
-    column_end(1, 2)
-    column_low(3, 0)
-    column_high(3, 0)
-    second_hop(3)
-    cycle_rows(0)
-    hops(0, 0, 1)
-    second_hop(2)
     column_low(2, -1)
     column_high(2, -1)
-    shared(1)
     column_low(2, 1)
     column_high(2, 1)
+    column_low(3, 0)
+    hops(0, 0, 1)
+    column_end(2, 0)
+    column_high(3, 0)
+    column_end(1, 2)
+    cycle_rows(0)
+    second_hop(3)
+    column_low(2, 2)
+    column_high(2, 2)
+    shared(1)
+    column_low(3, -1)
+    column_high(3, -1)
     product(1, 0)
     hops(0, 1, 1)
     hops(1, 0, 0)
-    column_end(2, 0)
-    column_low(3, -1)
-    column_high(3, -1)
+    column_end(2, -1)
+    hops(0, 0, 2)
+    column_end(2, 1)
     column_low(3, 1)
     column_high(3, 1)
-    hops(0, 0, 2)
     column_end(3, 0)
     column_low(3, 2)
+    column_end(2, 2)
     column_high(3, 2)
     product(1, 1)
     hops(1, 1, 0)
-    column_low(2, 2)
-    column_high(2, 2)
-    column_end(2, -1)
-    column_end(2, 1)
+    shared(2)
+    column_end(3, -1)
+    product(2, 0)
     hops(0, 1, 2)
-    column_end(3, -1)
-    cycle_rows(1)
+    hops(1, 0, 1)
+    hops(2, 0, 0)
     column_end(3, 1)
-    hops(1, 0, 1)
     column_end(3, 2)
-    hops(0, 0, 3)
+    product(2, 1)
+    hops(1, 1, 1)
+    hops(2, 1, 0)
     shared(3)
-    column_end(2, 2)
-    hops(1, 1, 1)
     product(3, 0)
-    hops(0, 1, 3)
-    hops(1, 0, 2)
     hops(3, 0, 0)
     product(3, 1)
+    hops(1, 0, 2)
+    hops(2, 0, 1)
     hops(3, 1, 0)
-    shared(2)
-    hops(1, 1, 2)
-    product(2, 0)
-    hops(1, 0, 3)
-    hops(2, 0, 0)
-    product(2, 1)
-    hops(2, 1, 0)
-    hops(3, 0, 1)
-    hops(3, 1, 1)
     settle(0, 0)
     settle(0, 1)
+    hops(1, 1, 2)
+    cycle_rows(1)
     cycle_rows(2)
-    hops(1, 1, 3)
+    hops(2, 1, 1)
     cycle_rows(3)
     cycle_product()
-    hops(2, 0, 1)
+    hops(3, 0, 1)
     settle(1, 0)
-    hops(2, 1, 1)
-    hops(3, 0, 2)
-    hops(3, 1, 2)
+    hops(2, 0, 2)
+    hops(3, 1, 1)
     cycle_spread()
     settle(1, 1)
-    hops(2, 0, 2)
     hops(2, 1, 2)
-    hops(3, 0, 3)
-    hops(3, 1, 3)
+    hops(3, 0, 2)
     hops(2, 0, 3)
+    hops(3, 1, 2)
     hops(2, 1, 3)
     cycle_settle()
     settle(3, 0)
+    settle(2, 0)
     settle(3, 1)
-    settle(2, 0)
     settle(2, 1)
     ladder_ref[...] = outf[...].astype(jnp.bfloat16)
     for copy in pending:
@@ -466,9 +480,10 @@
             jax.ShapeDtypeStruct((120, 1024), jnp.bfloat16),
             jax.ShapeDtypeStruct((16, 512), jnp.bfloat16),
         ),
-        in_specs=[any_space, any_space, any_space, pl.BlockSpec(memory_space=pltpu.SMEM)],
+        in_specs=[any_space, any_space, any_space, any_space],
         out_specs=(vmem, vmem),
         scratch_shapes=[
+            pltpu.SMEM((2, 8), jnp.int32),
             pltpu.VMEM((ROWS, 2 * HALF), jnp.bfloat16),
             pltpu.VMEM((STAGE * STAGES, 2 * HALF), jnp.bfloat16),
             pltpu.VMEM((STAGE * STAGES, 2 * HALF), jnp.bfloat16),
@@ -487,7 +502,7 @@
             pltpu.VMEM((16, 16, 512), jnp.float32),
             pltpu.VMEM((16, 16, 512), jnp.float32),
             pltpu.VMEM((15, 16, 512), jnp.float32),
-            dma((10,)),
+            dma((11,)),
             dma((2,)),
             dma((2,)),
             dma((STAGES, 20)),

time: 65.9 us -> 64.5 us (0.979)
  Pallas kernels: 65.1 us -> 63.7 us
    pallas_call x1, Pallas kernels: 63.4 us -> 62.1 us  [local(): pl.pallas_call(kernel, out_shape=(jax.ShapeDtypeStruct((120, 1024), jnp.b...]
where the time goes in v4:
time: 64.5 us; the launch traced here: 64.4 us
  Pallas kernels  63.7 us (99%)
    pallas_call x1, Pallas kernels, local(): pl.pallas_call(kernel, out_shape=(jax.ShapeDtypeStruct((120, 1024), jnp.b...  62.1 us
    pallas_call x1, Pallas kernels, local(): pl.pallas_call(hand_over, out_shape=(jax.ShapeDtypeStruct((120, 1024), jn...  1.66 us

profile of v4, /device:TPU:32, one launch (start us, length us, event | category | flops | bytes accessed | tf_op | source)
XLA Modules:
  0.0 64.4 jit_solution(1449556983528077278)
XLA Ops:
  0.6 62.1 %shard_map.59 = (bf16[120,1024]{1,0:T(8,128)(2,1)}, bf16[16,512]{1,0:T(8,128)(2,1)}) custom-call(bf16[30,4096]{1,0:T(8,128)(2,1)} %amp_hbm.1, bf16[4096,1024]{1,0:T(8,128)(2,1)} %ints_hbm.1, bf16[2,120,512]{2,1,0:T(8,128)(2,1)} %bitcast.3, s32[2,8]{1,0:T(2,128)} %bitcast.4), custom_call_target="tpu_custom_call" | custom-call | tf_op jit(solution)/shard_map/pallas_call | solution.py:477
  62.7 1.7 %shard_map.60 = (bf16[120,1024]{1,0:T(8,128)(2,1)}, bf16[16,512]{1,0:T(8,128)(2,1)}) custom-call(bf16[120,1024]{1,0:T(8,128)(2,1)} %get-tuple-element.6.ladder_in, bf16[16,512]{1,0:T(8,128)(2,1)} %get-tuple-element.7.cycle_in), custom_call_target="tpu_custom_call" | custom-call | tf_op jit(solution)/shard_map/pallas_call | solution.py:525

commit v5 on v4

--- a/solution.py
+++ b/solution.py
@@ -238,7 +238,7 @@
             v = chunk(h, half, dest, lb)
             for pieces in before:
                 v = v + pieces[lb]
-            top = jnp.maximum(jnp.max(jnp.abs(v), axis=0, keepdims=True), 1e-36)
+            top = jnp.maximum(jnp.max(jnp.abs(v), axis=0, keepdims=True), 1e-30)
             code = jnp.ceil(jnp.log2(top) * CODE)
             q = jnp.round(v * (jnp.exp2(code * (-1.0 / CODE)) * TOP))
             sbuf[h, way, half, slot, lb * CHUNK:(lb + 1) * CHUNK, :] = q.astype(jnp.int32).astype(jnp.int16)

time: 64.5 us -> 64.5 us (level)
  no operation moved by 1% of the time
where the time goes in v5:
time: 64.5 us; the launch traced here: 64.4 us
  Pallas kernels  63.7 us (99%)
    pallas_call x1, Pallas kernels, local(): pl.pallas_call(kernel, out_shape=(jax.ShapeDtypeStruct((120, 1024), jnp.b...  62.1 us
    pallas_call x1, Pallas kernels, local(): pl.pallas_call(hand_over, out_shape=(jax.ShapeDtypeStruct((120, 1024), jn...  1.66 us

profile of v5, /device:TPU:32, one launch (start us, length us, event | category | flops | bytes accessed | tf_op | source)
XLA Modules:
  0.0 64.4 jit_solution(4185410447181681338)
XLA Ops:
  0.6 62.1 %shard_map.59 = (bf16[120,1024]{1,0:T(8,128)(2,1)}, bf16[16,512]{1,0:T(8,128)(2,1)}) custom-call(bf16[30,4096]{1,0:T(8,128)(2,1)} %amp_hbm.1, bf16[4096,1024]{1,0:T(8,128)(2,1)} %ints_hbm.1, bf16[2,120,512]{2,1,0:T(8,128)(2,1)} %bitcast.3, s32[2,8]{1,0:T(2,128)} %bitcast.4), custom_call_target="tpu_custom_call" | custom-call | tf_op jit(solution)/shard_map/pallas_call | solution.py:477
  62.7 1.7 %shard_map.60 = (bf16[120,1024]{1,0:T(8,128)(2,1)}, bf16[16,512]{1,0:T(8,128)(2,1)}) custom-call(bf16[120,1024]{1,0:T(8,128)(2,1)} %get-tuple-element.6.ladder_in, bf16[16,512]{1,0:T(8,128)(2,1)} %get-tuple-element.7.cycle_in), custom_call_target="tpu_custom_call" | custom-call | tf_op jit(solution)/shard_map/pallas_call | solution.py:525
